TPU v7x, 32 devices: a whole 2x2x4 slice. The times are simulated.
32 devices in a mesh: tile: 4 (over y, core), slab: 8 (over z, x).
Axes of the slice: x: 2, y: 2, z: 4, core: 2. Of those that a mesh axis runs over, the one named last changes fastest.
Arguments:
- volume: float32 [256, 16384], P('slab', 'tile'), may hold values from -6 to 6
- measured: float32 [256, 8192], P('slab', 'tile'), may hold values from -6 to 6
- weights: float32 [256, 8192], P('slab', 'tile'), may hold values from 0.25 to 4
- footprints: float32 [1024, 32, 128], P('tile'), may hold values from -0.25 to 0.25
- foot_pixel: int32 [1024], P('tile'), may hold values from 0 to 31
- foot_strip: int32 [1024], P('tile'), may hold values from 0 to 255
Outputs:
- smoothed: float32 [256, 16384], P('slab', 'tile')
- residual: float32 [256, 8192], P('slab', 'tile')
Inputs may be any that keep to these rules, and one draw needn't show every extreme that they name: foot_pixel names one of the 32 pixel blocks of the tile that holds the footprint block. foot_strip names a strip of 32 rays.
All inputs are finite; a program needn't handle non-finite values.
Results may differ from a plain program's by a relative error of at most 0.0003.
Values sent between devices are 32-bit elements; how exact they have to be, the bound alone decides.
A program may use at most 64 MiB of HBM per device.

v0:
```python
import functools

import jax
import jax.numpy as jnp
from jax import lax
from jax.experimental import pallas as pl
from jax.experimental.pallas import tpu as pltpu
from jax.sharding import PartitionSpec as P

STRIPS = 256
PASSES = 3
LANES = 128
UNROLL = 8
MOST_CHUNKS = 4

huber_width = 0.5
smooth_rate = 0.2
MESH = pl.DeviceIdType.MESH
VMEM = pl.BlockSpec(memory_space=pltpu.VMEM)
SMEM = pl.BlockSpec(memory_space=pltpu.SMEM)
f32 = jnp.float32
bf16 = jnp.bfloat16


def halves(x):
    high = x.astype(bf16)
    return high, (x - high.astype(f32)).astype(bf16)


def triple(x):
    high, low = halves(x)
    return jnp.concatenate([high, low, high], axis=1)


def project(v3, fs, pix, strip, part):
    count, rows, _ = fs.shape
    slots = LANES // rows
    slices = v3.shape[1]
    slot_of = lax.broadcasted_iota(jnp.int32, (slices, LANES), 1) // rows
    part[...] = jnp.zeros_like(part)

    def step(i, carry):
        found = []
        for u in range(UNROLL):
            b = i * UNROLL + u
            q = strip[b]
            pair = fs[b]
            high, low = pair[:, :LANES], pair[:, LANES:]
            right = jnp.concatenate([jnp.concatenate([high, high, low], axis=1)] * slots, axis=0)
            out = lax.dot_general(
                v3[pix[b]], right, (((1,), (1,)), ((), ())), preferred_element_type=f32
            )
            found.append((q, jnp.where(slot_of == q % slots, out, 0.0)))
        for q, out in found:
            part[q // slots] += out
        return carry

    lax.fori_loop(0, count // UNROLL, step, 0)


def back(r3, mask, fs, pix, strip, grad):
    count, rows, _ = fs.shape
    slots = LANES // rows
    grad[...] = jnp.zeros_like(grad)

    def step(i, carry):
        found = []
        for u in range(UNROLL):
            b = i * UNROLL + u
            q = strip[b]
            pair = fs[b]
            high, low = pair[:, :LANES], pair[:, LANES:]
            right = jnp.concatenate([high] * (2 * slots) + [low] * slots, axis=0)
            left = r3[q // slots] * mask[q % slots]
            out = lax.dot_general(
                left, right, (((1,), (0,)), ((), ())), preferred_element_type=f32
            )
            found.append((pix[b], out))
        for p, out in found:
            grad[p] += out
        return carry

    lax.fori_loop(0, count // UNROLL, step, 0)


def fill_mask(mask, rows):
    slots, slices, wide = mask.shape
    slot_of = (lax.broadcasted_iota(jnp.int32, (slices, wide), 1) % LANES) // rows
    for slot in range(slots):
        mask[slot] = jnp.where(slot_of == slot, 1.0, 0.0).astype(bf16)


def first_kernel(pix, strip, volume, feet, fs, part, v3):
    count = feet.shape[0]
    for p in range(v3.shape[0]):
        v3[p] = triple(volume[:, p * LANES : (p + 1) * LANES])

    def split(i, carry):
        for u in range(UNROLL):
            b = i * UNROLL + u
            fs[b] = jnp.concatenate(halves(feet[b]), axis=1)
        return carry

    lax.fori_loop(0, count // UNROLL, split, 0)
    project(v3, fs, pix, strip, part)


def fold8(x):
    return jnp.sum(x.reshape(x.shape[0] // 8, 8, LANES), axis=0)


def load_rays(wr, r3):
    def one(g, carry):
        r3[g] = triple(wr[g])
        return carry

    lax.fori_loop(0, r3.shape[0], one, 0)


def middle_kernel(pix, strip, fs, wr, grad, part, square, v3, r3, mask):
    fill_mask(mask, fs.shape[1])
    load_rays(wr, r3)
    back(r3, mask, fs, pix, strip, grad)
    total = jnp.zeros((8, LANES), f32)
    for p in range(v3.shape[0]):
        value = grad[p]
        v3[p] = triple(value)
        total += fold8(value * value)
    square[...] = total
    project(v3, fs, pix, strip, part)


def last_kernel(pix, strip, fs, wr, first, volume, sums, grad, part, square, current, halo, v3, r3, mask):
    fill_mask(mask, fs.shape[1])
    load_rays(wr, r3)
    back(r3, mask, fs, pix, strip, grad)
    rate = jnp.sum(sums[0]) / jnp.sum(sums[1])
    slices = grad.shape[1]
    total = jnp.zeros((8, LANES), f32)
    for p in range(v3.shape[0]):
        value = first[p] - rate * grad[p]
        now = volume[:, p * LANES : (p + 1) * LANES] - rate * first[p]
        grad[p] = value
        current[p] = now
        v3[p] = triple(value)
        total += fold8(value * value)
    square[...] = total
    for which, source in enumerate((current, grad)):
        for row in range(PASSES):
            halo[0, which, row] = source[:, slices - PASSES + row, :]
            halo[1, which, row] = source[:, row, :]
    project(v3, fs, pix, strip, part)


def finish_kernel(current, grad, halo, sums, rate_sums, start, projected, later, smoothed, residual, ext):
    rate0 = jnp.sum(rate_sums[0]) / jnp.sum(rate_sums[1])
    rate1 = jnp.sum(sums[0]) / jnp.sum(sums[1])
    count, slices, _ = current.shape
    for g in range(start.shape[0]):
        residual[:, g * LANES : (g + 1) * LANES] = (
            start[g] - rate0 * projected[g] - rate1 * later[g]
        )
    tall = slices + 16
    first_row = lax.axis_index("slab") * slices - 8
    total_rows = slices * lax.axis_size("slab")
    row = first_row + lax.broadcasted_iota(jnp.int32, (tall, LANES), 0)
    linked = (row >= 0) & (row + 1 < total_rows)
    for p in range(count):
        ext[p, 0:8] = jnp.zeros((8, LANES), f32)
        ext[p, 8 : 8 + slices] = current[p] - rate1 * grad[p]
        ext[p, 8 + slices :] = jnp.zeros((8, LANES), f32)
    for i in range(PASSES):
        ext[:, 8 - PASSES + i, :] = halo[0, 0, i] - rate1 * halo[0, 1, i]
        ext[:, 8 + slices + i, :] = halo[1, 0, i] - rate1 * halo[1, 1, i]
    for p in range(count):
        value = ext[p]
        for number in range(PASSES):
            differ = jnp.clip(pltpu.roll(value, tall - 1, 0) - value, -huber_width, huber_width)
            clipped = jnp.where(linked, differ, 0.0)
            value = value + smooth_rate * (clipped - pltpu.roll(clipped, 1, 0))
        smoothed[:, p * LANES : (p + 1) * LANES] = value[8 : 8 + slices]


def exchange_kernel(mode, n, slabs, chunks, *refs):
    refs = list(refs)
    part = refs.pop(0)
    weights = refs.pop(0)
    measured = refs.pop(0) if mode == "first" else None
    square = refs.pop(0) if mode != "first" else None
    halo = refs.pop(0) if mode == "last" else None
    own = refs.pop(0)
    gathered = refs.pop(0) if mode != "last" else None
    sums = refs.pop(0) if mode != "first" else None
    halo_in = refs.pop(0) if mode == "last" else None
    near, chip_sum, far, near_s, near_r, far_s, far_r, ag_s, ag_r, sib_s, sib_r = refs[:11]
    refs = refs[11:]
    if mode != "first":
        mine, tile_in, slab_in, t_s, t_r, b_s, b_r = refs[:7]
        refs = refs[7:]
    if mode == "last":
        h_s, h_r = refs

    half = n // 2
    pieces = part.shape[2]
    size = pieces // chunks
    me = lax.axis_index("tile")
    slab = lax.axis_index("slab")
    par = lax.rem(me, 2)
    row = me // 2
    sibling = me + 1 - 2 * par
    started = []

    def at(tile):
        return {"tile": tile}

    def along(other):
        return {"slab": other}

    def peer(d):
        return lax.rem(row + d, half) * 2 + par

    def send(src, dst, s, r, where):
        copy = pltpu.make_async_remote_copy(
            src_ref=src, dst_ref=dst, send_sem=s, recv_sem=r, device_id=where, device_id_type=MESH
        )
        copy.start()
        started.append(copy)
        return copy

    barrier = pltpu.get_barrier_semaphore()
    greeted = 0
    if mode == "first":
        tiles = [sibling] + [peer(d) for d in range(1, half)]
    else:
        tiles = [lax.rem(me + d, n) for d in range(1, n)]
    for tile in tiles:
        pl.semaphore_signal(barrier, inc=1, device_id=at(tile), device_id_type=MESH)
        greeted += 1
    if mode != "first":
        for d in range(1, slabs):
            pl.semaphore_signal(
                barrier, inc=1, device_id=along(lax.rem(slab + d, slabs)), device_id_type=MESH
            )
            greeted += 1
    pl.semaphore_wait(barrier, greeted)

    spans = [pl.ds(c * size, size) for c in range(chunks)]
    first_hop = [
        send(part.at[:, 1 - par, span], near.at[:, span], near_s.at[c], near_r.at[c], at(sibling))
        for c, span in enumerate(spans)
    ]
    second_hop = []
    for c, span in enumerate(spans):
        first_hop[c].wait_recv()
        for g in range(c * size, (c + 1) * size):
            for o in range(half):
                chip_sum[o, g] = part[o, par, g] + near[o, g]
        second_hop.append(
            [
                send(
                    chip_sum.at[lax.rem(row + d, half), span],
                    far.at[d - 1, span],
                    far_s.at[c, d - 1],
                    far_r.at[c, d - 1],
                    at(peer(d)),
                )
                for d in range(1, half)
            ]
        )
    if mode == "last":
        up = send(halo.at[0], halo_in.at[0], h_s.at[0], h_r.at[0], along(lax.rem(slab + 1, slabs)))
        down = send(
            halo.at[1], halo_in.at[1], h_s.at[1], h_r.at[1], along(lax.rem(slab + slabs - 1, slabs))
        )
    curve = jnp.zeros((8, LANES), f32)
    across = []
    aside = []
    for c, span in enumerate(spans):
        for copy in second_hop[c]:
            copy.wait_recv()
        for g in range(c * size, (c + 1) * size):
            value = chip_sum[row, g]
            for d in range(1, half):
                value += far[d - 1, g]
            lanes = slice(g * LANES, (g + 1) * LANES)
            if mode == "first":
                value = value - measured[:, lanes]
            weighted = weights[:, lanes] * value
            own[g] = value
            if mode != "first":
                curve += fold8(weighted * value)
            if mode != "last":
                gathered[row, par, g] = weighted
        if mode != "last":
            spot = gathered.at[row, par, span]
            across.append(
                [
                    send(spot, spot, ag_s.at[c, d - 1], ag_r.at[c, d - 1], at(peer(d)))
                    for d in range(1, half)
                ]
            )
            aside.append(send(spot, spot, sib_s.at[0, c], sib_r.at[0, c], at(sibling)))
    if mode != "first":
        mine[0, 0] = square[...]
        mine[0, 1] = curve
        tile_copies = [
            send(
                mine.at[0],
                tile_in.at[d - 1],
                t_s.at[d - 1],
                t_r.at[d - 1],
                at(lax.rem(me + d, n)),
            )
            for d in range(1, n)
        ]
    if mode != "last":
        for c, span in enumerate(spans):
            for d in range(1, half):
                across[c][d - 1].wait_recv()
                spot = gathered.at[lax.rem(row + half - d, half), par, span]
                aside.append(send(spot, spot, sib_s.at[d, c], sib_r.at[d, c], at(sibling)))
    if mode != "first":
        total = mine[0]
        for d in range(1, n):
            tile_copies[d - 1].wait_recv()
            total += tile_in[d - 1]
        mine[1] = total
        slab_copies = [
            send(
                mine.at[1],
                slab_in.at[d - 1],
                b_s.at[d - 1],
                b_r.at[d - 1],
                along(lax.rem(slab + d, slabs)),
            )
            for d in range(1, slabs)
        ]
        for d in range(1, slabs):
            slab_copies[d - 1].wait_recv()
            total += slab_in[d - 1]
        sums[...] = total
    for copy in aside:
        copy.wait_recv()
    if mode == "last":
        up.wait_recv()
        down.wait_recv()
    for copy in started:
        copy.wait_send()


def exchange(mode, part, weights, extra, n, slabs, ident):
    groups, slices, _ = part.shape
    half, pieces = n // 2, groups // n
    chunks = max(c for c in range(1, MOST_CHUNKS + 1) if pieces % c == 0)
    shape = jax.ShapeDtypeStruct
    outs = [shape((pieces, slices, LANES), f32)]
    if mode != "last":
        outs.append(shape((half, 2, pieces, slices, LANES), f32))
    if mode != "first":
        outs.append(shape((2, 8, LANES), f32))
    if mode == "last":
        outs.append(shape(extra[1].shape, f32))
    dma = pltpu.SemaphoreType.DMA
    others = max(half - 1, 1)
    scratch = [
        pltpu.VMEM((half, pieces, slices, LANES), f32),
        pltpu.VMEM((half, pieces, slices, LANES), f32),
        pltpu.VMEM((others, pieces, slices, LANES), f32),
        dma((chunks,)),
        dma((chunks,)),
        dma((chunks, others)),
        dma((chunks, others)),
        dma((chunks, others)),
        dma((chunks, others)),
        dma((half, chunks)),
        dma((half, chunks)),
    ]
    if mode != "first":
        scratch += [
            pltpu.VMEM((2, 2, 8, LANES), f32),
            pltpu.VMEM((n - 1, 2, 8, LANES), f32),
            pltpu.VMEM((max(slabs - 1, 1), 2, 8, LANES), f32),
            dma((n - 1,)),
            dma((n - 1,)),
            dma((max(slabs - 1, 1),)),
            dma((max(slabs - 1, 1),)),
        ]
    if mode == "last":
        scratch += [dma((2,)), dma((2,))]
    inputs = [part.reshape(half, 2, pieces, slices, LANES), weights, *extra]
    return pl.pallas_call(
        functools.partial(exchange_kernel, mode, n, slabs, chunks),
        out_shape=outs,
        in_specs=[VMEM] * len(inputs),
        out_specs=[VMEM] * len(outs),
        scratch_shapes=scratch,
        compiler_params=pltpu.CompilerParams(collective_id=ident, has_side_effects=True),
        name="exchange_" + mode,
    )(*inputs)


def shards(n, slabs, volume, measured, weights, footprints, foot_pixel, foot_strip):
    slices = volume.shape[0]
    blocks = volume.shape[1] // LANES
    count, rows, _ = footprints.shape
    slots = LANES // rows
    groups = STRIPS // slots
    shape = jax.ShapeDtypeStruct
    part_shape = shape((groups, slices, LANES), f32)
    grad_shape = shape((blocks, slices, LANES), f32)
    v3 = pltpu.VMEM((blocks, slices, 3 * LANES), bf16)
    r3 = pltpu.VMEM((groups, slices, 3 * LANES), bf16)
    mask = pltpu.VMEM((slots, slices, 3 * LANES), bf16)

    def local(body, name, outs, scratch, *inputs):
        return pl.pallas_call(
            body,
            out_shape=outs,
            in_specs=[SMEM, SMEM] + [VMEM] * len(inputs),
            out_specs=[VMEM] * len(outs),
            scratch_shapes=scratch,
            name=name,
        )(foot_pixel, foot_strip, *inputs)

    fs, part = local(
        first_kernel,
        "project_first",
        [shape((count, rows, 2 * LANES), bf16), part_shape],
        [v3],
        volume,
        footprints,
    )
    start, wr = exchange("first", part, weights, [measured], n, slabs, 1)
    first, part, square = local(
        middle_kernel,
        "gradient_first",
        [grad_shape, part_shape, shape((8, LANES), f32)],
        [v3, r3, mask],
        fs,
        wr.reshape(groups, slices, LANES),
    )
    projected, wp, sums = exchange("middle", part, weights, [square], n, slabs, 2)
    halo_shape = shape((2, 2, PASSES, blocks, LANES), f32)
    grad, part, square, current, halo = local(
        last_kernel,
        "gradient_second",
        [grad_shape, part_shape, shape((8, LANES), f32), grad_shape, halo_shape],
        [v3, r3, mask],
        fs,
        wp.reshape(groups, slices, LANES),
        first,
        volume,
        sums,
    )
    later, last_sums, halo_in = exchange("last", part, weights, [square, halo], n, slabs, 3)
    return pl.pallas_call(
        finish_kernel,
        out_shape=[shape(volume.shape, f32), shape(measured.shape, f32)],
        in_specs=[VMEM] * 8,
        out_specs=[VMEM] * 2,
        scratch_shapes=[pltpu.VMEM((blocks, slices + 16, LANES), f32)],
        name="smooth",
    )(current, grad, halo_in, last_sums, sums, start, projected, later)


def solution(mesh):
    return jax.shard_map(
        functools.partial(shards, mesh.shape["tile"], mesh.shape["slab"]),
        mesh=mesh,
        in_specs=(
            P("slab", "tile"),
            P("slab", "tile"),
            P("slab", "tile"),
            P("tile", None, None),
            P("tile"),
            P("tile"),
        ),
        out_specs=(P("slab", "tile"), P("slab", "tile")),
        check_vma=False,
    )
```

profile of v0, /device:TPU:0, one launch (start us, length us, event | category | flops | bytes accessed | tf_op | source)
XLA Modules:
  0.0 139.7 jit_solution(2987114950137431059)
XLA Ops:
  0.6 18.0 %project_first.1 = (bf16[256,32,256]{2,1,0:T(8,128)(2,1)}, f32[64,32,128]{2,1,0:T(8,128)}) custom-call(s32[256]{0:T(256)} %pix.5, s32[256]{0:T(256)} %strip.5, f32[32,4096]{1,0:T(8,128)} %volume.3, f32[256,32,128]{2,1,0:T(8,128)} %feet.1), custom_call_target="tpu_custom_call" | custom-call | tf_op jit(solution)/shard_map/project_first/pallas_call | solution.py:416
  18.6 20.1 %exchange_first.1 = (f32[16,32,128]{2,1,0:T(8,128)}, f32[2,2,16,32,128]{4,3,2,1,0:T(8,128)}) custom-call(f32[2,2,16,32,128]{4,3,2,1,0:T(8,128)} %bitcast.7, f32[32,2048]{1,0:T(8,128)} %refs_1_.5, f32[32,2048]{1,0:T(8,128)} %refs_2_.1), custom_call_target="tpu_custom_call" | custom-call | tf_op jit(solution)/shard_map/exchange_first/pallas_call | solution.py:391
  38.8 25.2 %gradient_first.1 = (f32[32,32,128]{2,1,0:T(8,128)}, f32[64,32,128]{2,1,0:T(8,128)}, f32[8,128]{1,0:T(8,128)}) custom-call(s32[256]{0:T(256)} %pix.5, s32[256]{0:T(256)} %strip.5, bf16[256,32,256]{2,1,0:T(8,128)(2,1)} %get-tuple-element.20.fs, f32[64,32,128]{2,1,0:T(8,128)} %bitcast.5), custom_call_target="tpu_custom_call" | custom-call | tf_op jit(solution)/shard_map/gradient_first/pallas_call | solution.py:416
  64.0 25.4 %exchange_middle.1 = (f32[16,32,128]{2,1,0:T(8,128)}, f32[2,2,16,32,128]{4,3,2,1,0:T(8,128)}, f32[2,8,128]{2,1,0:T(8,128)}) custom-call(f32[2,2,16,32,128]{4,3,2,1,0:T(8,128)} %bitcast.6, f32[32,2048]{1,0:T(8,128)} %refs_1_.5, f32[8,128]{1,0:T(8,128)} %get-tuple-element.24.refs_2_), custom_call_target="tpu_custom_call" | custom-call | tf_op jit(solution)/shard_map/exchange_middle/pallas_call | solution.py:391
  89.5 25.9 %gradient_second.1 = (f32[32,32,128]{2,1,0:T(8,128)}, f32[64,32,128]{2,1,0:T(8,128)}, f32[8,128]{1,0:T(8,128)}, f32[32,32,128]{2,1,0:T(8,128)}, f32[2,2,3,32,128]{4,3,2,1,0:T(8,128)}) custom-call(s32[256]{0:T(256)} %pix.5, s32[256]{0:T(256)} %strip.5, bf16[256,32,256]{2,1,0:T(8,128)(2,1)} %get-tuple-element.20.fs, f32[64,32,128]{2,1,0:T(8,128)} %bitcast.9, ...), custom_call_target="tpu_custom_call" | custom-call | tf_op jit(solution)/shard_map/gradient_second/pallas_call | solution.py:416
  115.4 21.0 %exchange_last.1 = (f32[16,32,128]{2,1,0:T(8,128)}, f32[2,8,128]{2,1,0:T(8,128)}, f32[2,2,3,32,128]{4,3,2,1,0:T(8,128)}) custom-call(f32[2,2,16,32,128]{4,3,2,1,0:T(8,128)} %bitcast.8, f32[32,2048]{1,0:T(8,128)} %refs_1_.5, f32[8,128]{1,0:T(8,128)} %get-tuple-element.31.refs_2_, f32[2,2,3,32,128]{4,3,2,1,0:T(8,128)} %get-tuple-element.32.refs_3_), custom_call_target="tpu_custom_call" | custom-call | tf_op jit(solution)/shard_map/exchange_last/pallas_call | solution.py:391
  136.4 3.4 %smooth.1 = (f32[32,4096]{1,0:T(8,128)}, f32[32,2048]{1,0:T(8,128)}) custom-call(f32[32,32,128]{2,1,0:T(8,128)} %get-tuple-element.28.current, f32[32,32,128]{2,1,0:T(8,128)} %get-tuple-element.29.grad, f32[2,2,3,32,128]{4,3,2,1,0:T(8,128)} %get-tuple-element.33.halo, f32[2,8,128]{2,1,0:T(8,128)} %get-tuple-element.34.sums, ...), custom_call_target="tpu_custom_call" | custom-call | tf_op jit(solution)/shard_map/smooth/pallas_call | solution.py:456
where the time goes:
time: 140 us
  Pallas kernels  139 us (99%)
    pallas_call x3, Pallas kernels, local(): pl.pallas_call(body, out_shape=outs, in_specs=[SMEM, SMEM] + [VMEM] * len...  69.2 us
    pallas_call x3, Pallas kernels, exchange(): pl.pallas_call(functools.partial(exchange_kernel, mode, n, slabs, chunks)...  66.5 us
    pallas_call x1, Pallas kernels, shards(): pl.pallas_call(finish_kernel, out_shape=[shape(volume.shape, f32), shape(...  3.38 us

commit v1 on v0

--- a/solution.py
+++ b/solution.py
@@ -10,7 +10,7 @@
 STRIPS = 256
 PASSES = 3
 LANES = 128
-UNROLL = 8
+UNROLL = 2
 MOST_CHUNKS = 4
 
 huber_width = 0.5
@@ -33,75 +33,84 @@
 
 
 def project(v3, fs, pix, strip, part):
-    count, rows, _ = fs.shape
-    slots = LANES // rows
     slices = v3.shape[1]
+    slots = pix.shape[0] // fs.shape[0]
+    rows = LANES // slots
     slot_of = lax.broadcasted_iota(jnp.int32, (slices, LANES), 1) // rows
     part[...] = jnp.zeros_like(part)
 
     def step(i, carry):
         found = []
         for u in range(UNROLL):
-            b = i * UNROLL + u
-            q = strip[b]
-            pair = fs[b]
+            t = i * UNROLL + u
+            pair = fs[t]
             high, low = pair[:, :LANES], pair[:, LANES:]
-            right = jnp.concatenate([jnp.concatenate([high, high, low], axis=1)] * slots, axis=0)
+            right = jnp.concatenate([high, high, low], axis=1)
+            left = jnp.concatenate([v3[pix[t * slots + k]] for k in range(slots)], axis=0)
             out = lax.dot_general(
-                v3[pix[b]], right, (((1,), (1,)), ((), ())), preferred_element_type=f32
-            )
-            found.append((q, jnp.where(slot_of == q % slots, out, 0.0)))
-        for q, out in found:
-            part[q // slots] += out
+                left, right, (((1,), (1,)), ((), ())), preferred_element_type=f32
+            )
+            for k in range(slots):
+                q = strip[t * slots + k]
+                own = q % slots
+                turned = pltpu.roll(
+                    out[k * slices : (k + 1) * slices], ((own - k + slots) % slots) * rows, 1
+                )
+                found.append((q // slots, jnp.where(slot_of == own, turned, 0.0)))
+        for g, out in found:
+            part[g] += out
         return carry
 
-    lax.fori_loop(0, count // UNROLL, step, 0)
-
-
-def back(r3, mask, fs, pix, strip, grad):
-    count, rows, _ = fs.shape
-    slots = LANES // rows
+    lax.fori_loop(0, fs.shape[0] // UNROLL, step, 0)
+
+
+def back(wr, fs, pix, strip, grad):
+    slices = wr.shape[1]
+    slots = pix.shape[0] // fs.shape[0]
+    rows = LANES // slots
+    slot_of = lax.broadcasted_iota(jnp.int32, (slices, LANES), 1) // rows
     grad[...] = jnp.zeros_like(grad)
 
     def step(i, carry):
         found = []
         for u in range(UNROLL):
-            b = i * UNROLL + u
-            q = strip[b]
-            pair = fs[b]
+            t = i * UNROLL + u
+            pair = fs[t]
             high, low = pair[:, :LANES], pair[:, LANES:]
-            right = jnp.concatenate([high] * (2 * slots) + [low] * slots, axis=0)
-            left = r3[q // slots] * mask[q % slots]
+            right = jnp.concatenate([high, high, low], axis=0)
+            left = []
+            for k in range(slots):
+                q = strip[t * slots + k]
+                turned = pltpu.roll(
+                    wr[q // slots], ((k - q % slots + slots) % slots) * rows, 1
+                )
+                left.append(triple(jnp.where(slot_of == k, turned, 0.0)))
             out = lax.dot_general(
-                left, right, (((1,), (0,)), ((), ())), preferred_element_type=f32
-            )
-            found.append((pix[b], out))
+                jnp.concatenate(left, axis=0),
+                right,
+                (((1,), (0,)), ((), ())),
+                preferred_element_type=f32,
+            )
+            for k in range(slots):
+                found.append((pix[t * slots + k], out[k * slices : (k + 1) * slices]))
         for p, out in found:
             grad[p] += out
         return carry
 
-    lax.fori_loop(0, count // UNROLL, step, 0)
-
-
-def fill_mask(mask, rows):
-    slots, slices, wide = mask.shape
-    slot_of = (lax.broadcasted_iota(jnp.int32, (slices, wide), 1) % LANES) // rows
-    for slot in range(slots):
-        mask[slot] = jnp.where(slot_of == slot, 1.0, 0.0).astype(bf16)
+    lax.fori_loop(0, fs.shape[0] // UNROLL, step, 0)
 
 
 def first_kernel(pix, strip, volume, feet, fs, part, v3):
-    count = feet.shape[0]
     for p in range(v3.shape[0]):
         v3[p] = triple(volume[:, p * LANES : (p + 1) * LANES])
 
     def split(i, carry):
         for u in range(UNROLL):
-            b = i * UNROLL + u
-            fs[b] = jnp.concatenate(halves(feet[b]), axis=1)
+            t = i * UNROLL + u
+            fs[t] = jnp.concatenate(halves(feet[t]), axis=1)
         return carry
 
-    lax.fori_loop(0, count // UNROLL, split, 0)
+    lax.fori_loop(0, feet.shape[0] // UNROLL, split, 0)
     project(v3, fs, pix, strip, part)
 
 
@@ -109,18 +118,8 @@
     return jnp.sum(x.reshape(x.shape[0] // 8, 8, LANES), axis=0)
 
 
-def load_rays(wr, r3):
-    def one(g, carry):
-        r3[g] = triple(wr[g])
-        return carry
-
-    lax.fori_loop(0, r3.shape[0], one, 0)
-
-
-def middle_kernel(pix, strip, fs, wr, grad, part, square, v3, r3, mask):
-    fill_mask(mask, fs.shape[1])
-    load_rays(wr, r3)
-    back(r3, mask, fs, pix, strip, grad)
+def middle_kernel(pix, strip, fs, wr, grad, part, square, v3):
+    back(wr, fs, pix, strip, grad)
     total = jnp.zeros((8, LANES), f32)
     for p in range(v3.shape[0]):
         value = grad[p]
@@ -130,10 +129,8 @@
     project(v3, fs, pix, strip, part)
 
 
-def last_kernel(pix, strip, fs, wr, first, volume, sums, grad, part, square, current, halo, v3, r3, mask):
-    fill_mask(mask, fs.shape[1])
-    load_rays(wr, r3)
-    back(r3, mask, fs, pix, strip, grad)
+def last_kernel(pix, strip, fs, wr, first, volume, sums, grad, part, square, current, halo, v3):
+    back(wr, fs, pix, strip, grad)
     rate = jnp.sum(sums[0]) / jnp.sum(sums[1])
     slices = grad.shape[1]
     total = jnp.zeros((8, LANES), f32)
@@ -409,8 +406,6 @@
     part_shape = shape((groups, slices, LANES), f32)
     grad_shape = shape((blocks, slices, LANES), f32)
     v3 = pltpu.VMEM((blocks, slices, 3 * LANES), bf16)
-    r3 = pltpu.VMEM((groups, slices, 3 * LANES), bf16)
-    mask = pltpu.VMEM((slots, slices, 3 * LANES), bf16)
 
     def local(body, name, outs, scratch, *inputs):
         return pl.pallas_call(
@@ -425,17 +420,17 @@
     fs, part = local(
         first_kernel,
         "project_first",
-        [shape((count, rows, 2 * LANES), bf16), part_shape],
+        [shape((count // slots, LANES, 2 * LANES), bf16), part_shape],
         [v3],
         volume,
-        footprints,
+        footprints.reshape(count // slots, LANES, LANES),
     )
     start, wr = exchange("first", part, weights, [measured], n, slabs, 1)
     first, part, square = local(
         middle_kernel,
         "gradient_first",
         [grad_shape, part_shape, shape((8, LANES), f32)],
-        [v3, r3, mask],
+        [v3],
         fs,
         wr.reshape(groups, slices, LANES),
     )
@@ -445,7 +440,7 @@
         last_kernel,
         "gradient_second",
         [grad_shape, part_shape, shape((8, LANES), f32), grad_shape, halo_shape],
-        [v3, r3, mask],
+        [v3],
         fs,
         wp.reshape(groups, slices, LANES),
         first,

time: 140 us -> 131 us (0.936)
  Pallas kernels: 139 us -> 130 us
    pallas_call x3, Pallas kernels: 69.2 us -> 60.4 us  [local(): pl.pallas_call(body, out_shape=outs, in_specs=[SMEM, SMEM] + [VMEM] * len...]
where the time goes in v1:
time: 131 us
  Pallas kernels  130 us (99%)
    pallas_call x3, Pallas kernels, exchange(): pl.pallas_call(functools.partial(exchange_kernel, mode, n, slabs, chunks)...  66.5 us
    pallas_call x3, Pallas kernels, local(): pl.pallas_call(body, out_shape=outs, in_specs=[SMEM, SMEM] + [VMEM] * len...  60.4 us
    pallas_call x1, Pallas kernels, shards(): pl.pallas_call(finish_kernel, out_shape=[shape(volume.shape, f32), shape(...  3.38 us

profile of v1, /device:TPU:0, one launch (start us, length us, event | category | flops | bytes accessed | tf_op | source)
XLA Modules:
  0.0 130.9 jit_solution(8076323526308956340)
XLA Ops:
  0.6 15.0 %project_first.1 = (bf16[64,128,256]{2,1,0:T(8,128)(2,1)}, f32[64,32,128]{2,1,0:T(8,128)}) custom-call(s32[256]{0:T(256)} %pix.5, s32[256]{0:T(256)} %strip.5, f32[32,4096]{1,0:T(8,128)} %volume.3, f32[64,128,128]{2,1,0:T(8,128)} %bitcast.6), custom_call_target="tpu_custom_call" | custom-call | tf_op jit(solution)/shard_map/project_first/pallas_call | solution.py:411
  15.6 20.1 %exchange_first.1 = (f32[16,32,128]{2,1,0:T(8,128)}, f32[2,2,16,32,128]{4,3,2,1,0:T(8,128)}) custom-call(f32[2,2,16,32,128]{4,3,2,1,0:T(8,128)} %bitcast.9, f32[32,2048]{1,0:T(8,128)} %refs_1_.5, f32[32,2048]{1,0:T(8,128)} %refs_2_.1), custom_call_target="tpu_custom_call" | custom-call | tf_op jit(solution)/shard_map/exchange_first/pallas_call | solution.py:388
  35.8 22.3 %gradient_first.1 = (f32[32,32,128]{2,1,0:T(8,128)}, f32[64,32,128]{2,1,0:T(8,128)}, f32[8,128]{1,0:T(8,128)}) custom-call(s32[256]{0:T(256)} %pix.5, s32[256]{0:T(256)} %strip.5, bf16[64,128,256]{2,1,0:T(8,128)(2,1)} %get-tuple-element.20.fs, f32[64,32,128]{2,1,0:T(8,128)} %bitcast.7), custom_call_target="tpu_custom_call" | custom-call | tf_op jit(solution)/shard_map/gradient_first/pallas_call | solution.py:411
  58.0 25.4 %exchange_middle.1 = (f32[16,32,128]{2,1,0:T(8,128)}, f32[2,2,16,32,128]{4,3,2,1,0:T(8,128)}, f32[2,8,128]{2,1,0:T(8,128)}) custom-call(f32[2,2,16,32,128]{4,3,2,1,0:T(8,128)} %bitcast.8, f32[32,2048]{1,0:T(8,128)} %refs_1_.5, f32[8,128]{1,0:T(8,128)} %get-tuple-element.24.refs_2_), custom_call_target="tpu_custom_call" | custom-call | tf_op jit(solution)/shard_map/exchange_middle/pallas_call | solution.py:388
  83.5 23.1 %gradient_second.1 = (f32[32,32,128]{2,1,0:T(8,128)}, f32[64,32,128]{2,1,0:T(8,128)}, f32[8,128]{1,0:T(8,128)}, f32[32,32,128]{2,1,0:T(8,128)}, f32[2,2,3,32,128]{4,3,2,1,0:T(8,128)}) custom-call(s32[256]{0:T(256)} %pix.5, s32[256]{0:T(256)} %strip.5, bf16[64,128,256]{2,1,0:T(8,128)(2,1)} %get-tuple-element.20.fs, f32[64,32,128]{2,1,0:T(8,128)} %bitcast.11, ...), custom_call_target="tpu_custom_call" | custom-call | tf_op jit(solution)/shard_map/gradient_second/pallas_call | solution.py:411
  106.6 21.0 %exchange_last.1 = (f32[16,32,128]{2,1,0:T(8,128)}, f32[2,8,128]{2,1,0:T(8,128)}, f32[2,2,3,32,128]{4,3,2,1,0:T(8,128)}) custom-call(f32[2,2,16,32,128]{4,3,2,1,0:T(8,128)} %bitcast.10, f32[32,2048]{1,0:T(8,128)} %refs_1_.5, f32[8,128]{1,0:T(8,128)} %get-tuple-element.31.refs_2_, f32[2,2,3,32,128]{4,3,2,1,0:T(8,128)} %get-tuple-element.32.refs_3_), custom_call_target="tpu_custom_call" | custom-call | tf_op jit(solution)/shard_map/exchange_last/pallas_call | solution.py:388
  127.6 3.4 %smooth.1 = (f32[32,4096]{1,0:T(8,128)}, f32[32,2048]{1,0:T(8,128)}) custom-call(f32[32,32,128]{2,1,0:T(8,128)} %get-tuple-element.28.current, f32[32,32,128]{2,1,0:T(8,128)} %get-tuple-element.29.grad, f32[2,2,3,32,128]{4,3,2,1,0:T(8,128)} %get-tuple-element.33.halo, f32[2,8,128]{2,1,0:T(8,128)} %get-tuple-element.34.sums, ...), custom_call_target="tpu_custom_call" | custom-call | tf_op jit(solution)/shard_map/smooth/pallas_call | solution.py:451

commit v2 on v1

--- a/solution.py
+++ b/solution.py
@@ -10,7 +10,7 @@
 STRIPS = 256
 PASSES = 3
 LANES = 128
-UNROLL = 2
+UNROLL = 16
 MOST_CHUNKS = 4
 
 huber_width = 0.5

time: 131 us -> 103 us (0.79)
  Pallas kernels: 130 us -> 102 us
    pallas_call x3, Pallas kernels: 60.4 us -> 31.8 us  [local(): pl.pallas_call(body, out_shape=outs, in_specs=[SMEM, SMEM] + [VMEM] * len...]
where the time goes in v2:
time: 103 us; the launch traced here: 102 us
  Pallas kernels  102 us (99%)
    pallas_call x3, Pallas kernels, exchange(): pl.pallas_call(functools.partial(exchange_kernel, mode, n, slabs, chunks)...  66.6 us
    pallas_call x3, Pallas kernels, local(): pl.pallas_call(body, out_shape=outs, in_specs=[SMEM, SMEM] + [VMEM] * len...  31.8 us
    pallas_call x1, Pallas kernels, shards(): pl.pallas_call(finish_kernel, out_shape=[shape(volume.shape, f32), shape(...  3.38 us

profile of v2, /device:TPU:0, one launch (start us, length us, event | category | flops | bytes accessed | tf_op | source)
XLA Modules:
  0.0 102.4 jit_solution(4784146914359958494)
XLA Ops:
  0.6 9.0 %project_first.1 = (bf16[64,128,256]{2,1,0:T(8,128)(2,1)}, f32[64,32,128]{2,1,0:T(8,128)}) custom-call(s32[256]{0:T(256)} %pix.5, s32[256]{0:T(256)} %strip.5, f32[32,4096]{1,0:T(8,128)} %volume.3, f32[64,128,128]{2,1,0:T(8,128)} %bitcast.6), custom_call_target="tpu_custom_call" | custom-call | tf_op jit(solution)/shard_map/project_first/pallas_call | solution.py:411
  9.6 20.2 %exchange_first.1 = (f32[16,32,128]{2,1,0:T(8,128)}, f32[2,2,16,32,128]{4,3,2,1,0:T(8,128)}) custom-call(f32[2,2,16,32,128]{4,3,2,1,0:T(8,128)} %bitcast.9, f32[32,2048]{1,0:T(8,128)} %refs_1_.5, f32[32,2048]{1,0:T(8,128)} %refs_2_.1), custom_call_target="tpu_custom_call" | custom-call | tf_op jit(solution)/shard_map/exchange_first/pallas_call | solution.py:388
  29.8 11.0 %gradient_first.1 = (f32[32,32,128]{2,1,0:T(8,128)}, f32[64,32,128]{2,1,0:T(8,128)}, f32[8,128]{1,0:T(8,128)}) custom-call(s32[256]{0:T(256)} %pix.5, s32[256]{0:T(256)} %strip.5, bf16[64,128,256]{2,1,0:T(8,128)(2,1)} %get-tuple-element.20.fs, f32[64,32,128]{2,1,0:T(8,128)} %bitcast.7), custom_call_target="tpu_custom_call" | custom-call | tf_op jit(solution)/shard_map/gradient_first/pallas_call | solution.py:411
  40.8 25.4 %exchange_middle.1 = (f32[16,32,128]{2,1,0:T(8,128)}, f32[2,2,16,32,128]{4,3,2,1,0:T(8,128)}, f32[2,8,128]{2,1,0:T(8,128)}) custom-call(f32[2,2,16,32,128]{4,3,2,1,0:T(8,128)} %bitcast.8, f32[32,2048]{1,0:T(8,128)} %refs_1_.5, f32[8,128]{1,0:T(8,128)} %get-tuple-element.24.refs_2_), custom_call_target="tpu_custom_call" | custom-call | tf_op jit(solution)/shard_map/exchange_middle/pallas_call | solution.py:388
  66.2 11.8 %gradient_second.1 = (f32[32,32,128]{2,1,0:T(8,128)}, f32[64,32,128]{2,1,0:T(8,128)}, f32[8,128]{1,0:T(8,128)}, f32[32,32,128]{2,1,0:T(8,128)}, f32[2,2,3,32,128]{4,3,2,1,0:T(8,128)}) custom-call(s32[256]{0:T(256)} %pix.5, s32[256]{0:T(256)} %strip.5, bf16[64,128,256]{2,1,0:T(8,128)(2,1)} %get-tuple-element.20.fs, f32[64,32,128]{2,1,0:T(8,128)} %bitcast.11, ...), custom_call_target="tpu_custom_call" | custom-call | tf_op jit(solution)/shard_map/gradient_second/pallas_call | solution.py:411
  78.0 21.0 %exchange_last.1 = (f32[16,32,128]{2,1,0:T(8,128)}, f32[2,8,128]{2,1,0:T(8,128)}, f32[2,2,3,32,128]{4,3,2,1,0:T(8,128)}) custom-call(f32[2,2,16,32,128]{4,3,2,1,0:T(8,128)} %bitcast.10, f32[32,2048]{1,0:T(8,128)} %refs_1_.5, f32[8,128]{1,0:T(8,128)} %get-tuple-element.31.refs_2_, f32[2,2,3,32,128]{4,3,2,1,0:T(8,128)} %get-tuple-element.32.refs_3_), custom_call_target="tpu_custom_call" | custom-call | tf_op jit(solution)/shard_map/exchange_last/pallas_call | solution.py:388
  99.0 3.4 %smooth.1 = (f32[32,4096]{1,0:T(8,128)}, f32[32,2048]{1,0:T(8,128)}) custom-call(f32[32,32,128]{2,1,0:T(8,128)} %get-tuple-element.28.current, f32[32,32,128]{2,1,0:T(8,128)} %get-tuple-element.29.grad, f32[2,2,3,32,128]{4,3,2,1,0:T(8,128)} %get-tuple-element.33.halo, f32[2,8,128]{2,1,0:T(8,128)} %get-tuple-element.34.sums, ...), custom_call_target="tpu_custom_call" | custom-call | tf_op jit(solution)/shard_map/smooth/pallas_call | solution.py:451

commit v3 on v2

--- a/solution.py
+++ b/solution.py
@@ -52,11 +52,18 @@
             )
             for k in range(slots):
                 q = strip[t * slots + k]
-                own = q % slots
+                own = lax.bitwise_and(q, slots - 1)
                 turned = pltpu.roll(
-                    out[k * slices : (k + 1) * slices], ((own - k + slots) % slots) * rows, 1
+                    out[k * slices : (k + 1) * slices],
+                    lax.bitwise_and(own + (slots - k), slots - 1) * rows,
+                    1,
                 )
-                found.append((q // slots, jnp.where(slot_of == own, turned, 0.0)))
+                found.append(
+                    (
+                        lax.shift_right_logical(q, slots.bit_length() - 1),
+                        jnp.where(slot_of == own, turned, 0.0),
+                    )
+                )
         for g, out in found:
             part[g] += out
         return carry
@@ -82,7 +89,9 @@
             for k in range(slots):
                 q = strip[t * slots + k]
                 turned = pltpu.roll(
-                    wr[q // slots], ((k - q % slots + slots) % slots) * rows, 1
+                    wr[lax.shift_right_logical(q, slots.bit_length() - 1)],
+                    lax.bitwise_and(k + slots - lax.bitwise_and(q, slots - 1), slots - 1) * rows,
+                    1,
                 )
                 left.append(triple(jnp.where(slot_of == k, turned, 0.0)))
             out = lax.dot_general(
@@ -129,30 +138,31 @@
     project(v3, fs, pix, strip, part)
 
 
-def last_kernel(pix, strip, fs, wr, first, volume, sums, grad, part, square, current, halo, v3):
+def last_kernel(pix, strip, fs, wr, first, volume, grad, part, halo, v3):
     back(wr, fs, pix, strip, grad)
-    rate = jnp.sum(sums[0]) / jnp.sum(sums[1])
     slices = grad.shape[1]
-    total = jnp.zeros((8, LANES), f32)
-    for p in range(v3.shape[0]):
-        value = first[p] - rate * grad[p]
-        now = volume[:, p * LANES : (p + 1) * LANES] - rate * first[p]
-        grad[p] = value
-        current[p] = now
-        v3[p] = triple(value)
-        total += fold8(value * value)
-    square[...] = total
-    for which, source in enumerate((current, grad)):
-        for row in range(PASSES):
-            halo[0, which, row] = source[:, slices - PASSES + row, :]
-            halo[1, which, row] = source[:, row, :]
+    blocks = v3.shape[0]
+    for p in range(blocks):
+        v3[p] = triple(grad[p])
+    for row in range(PASSES):
+        for side, spot in enumerate((slices - PASSES + row, row)):
+            for p in range(blocks):
+                halo[side, 0, row, p : p + 1] = volume[
+                    spot : spot + 1, p * LANES : (p + 1) * LANES
+                ]
+            halo[side, 1, row] = first[:, spot, :]
+            halo[side, 2, row] = grad[:, spot, :]
     project(v3, fs, pix, strip, part)
 
 
-def finish_kernel(current, grad, halo, sums, rate_sums, start, projected, later, smoothed, residual, ext):
-    rate0 = jnp.sum(rate_sums[0]) / jnp.sum(rate_sums[1])
-    rate1 = jnp.sum(sums[0]) / jnp.sum(sums[1])
-    count, slices, _ = current.shape
+def finish_kernel(volume, first, turned, halo, sums, start, projected, later, smoothed, residual, ext):
+    rate0 = jnp.sum(sums[0, 0]) / jnp.sum(sums[0, 1])
+    rate1 = jnp.sum(sums[1, 0]) / jnp.sum(sums[1, 1])
+
+    def stepped(image, one, two):
+        return image - rate0 * one - rate1 * (one - rate0 * two)
+
+    count, slices, _ = first.shape
     for g in range(start.shape[0]):
         residual[:, g * LANES : (g + 1) * LANES] = (
             start[g] - rate0 * projected[g] - rate1 * later[g]
@@ -164,11 +174,13 @@
     linked = (row >= 0) & (row + 1 < total_rows)
     for p in range(count):
         ext[p, 0:8] = jnp.zeros((8, LANES), f32)
-        ext[p, 8 : 8 + slices] = current[p] - rate1 * grad[p]
+        ext[p, 8 : 8 + slices] = stepped(
+            volume[:, p * LANES : (p + 1) * LANES], first[p], turned[p]
+        )
         ext[p, 8 + slices :] = jnp.zeros((8, LANES), f32)
     for i in range(PASSES):
-        ext[:, 8 - PASSES + i, :] = halo[0, 0, i] - rate1 * halo[0, 1, i]
-        ext[:, 8 + slices + i, :] = halo[1, 0, i] - rate1 * halo[1, 1, i]
+        ext[:, 8 - PASSES + i, :] = stepped(halo[0, 0, i], halo[0, 1, i], halo[0, 2, i])
+        ext[:, 8 + slices + i, :] = stepped(halo[1, 0, i], halo[1, 1, i], halo[1, 2, i])
     for p in range(count):
         value = ext[p]
         for number in range(PASSES):
@@ -183,19 +195,17 @@
     part = refs.pop(0)
     weights = refs.pop(0)
     measured = refs.pop(0) if mode == "first" else None
-    square = refs.pop(0) if mode != "first" else None
-    halo = refs.pop(0) if mode == "last" else None
+    if mode == "last":
+        projected, square, first, turned, halo = refs[:5]
+        refs = refs[5:]
     own = refs.pop(0)
     gathered = refs.pop(0) if mode != "last" else None
-    sums = refs.pop(0) if mode != "first" else None
+    sums = refs.pop(0) if mode == "last" else None
     halo_in = refs.pop(0) if mode == "last" else None
     near, chip_sum, far, near_s, near_r, far_s, far_r, ag_s, ag_r, sib_s, sib_r = refs[:11]
     refs = refs[11:]
-    if mode != "first":
-        mine, tile_in, slab_in, t_s, t_r, b_s, b_r = refs[:7]
-        refs = refs[7:]
-    if mode == "last":
-        h_s, h_r = refs
+    if mode == "last":
+        mine, tile_in, slab_in, t_s, t_r, b_s, b_r, h_s, h_r = refs
 
     half = n // 2
     pieces = part.shape[2]
@@ -226,14 +236,14 @@
 
     barrier = pltpu.get_barrier_semaphore()
     greeted = 0
-    if mode == "first":
+    if mode != "last":
         tiles = [sibling] + [peer(d) for d in range(1, half)]
     else:
         tiles = [lax.rem(me + d, n) for d in range(1, n)]
     for tile in tiles:
         pl.semaphore_signal(barrier, inc=1, device_id=at(tile), device_id_type=MESH)
         greeted += 1
-    if mode != "first":
+    if mode == "last":
         for d in range(1, slabs):
             pl.semaphore_signal(
                 barrier, inc=1, device_id=along(lax.rem(slab + d, slabs)), device_id_type=MESH
@@ -246,6 +256,55 @@
         send(part.at[:, 1 - par, span], near.at[:, span], near_s.at[c], near_r.at[c], at(sibling))
         for c, span in enumerate(spans)
     ]
+    def tile_round(k, top, bottom):
+        mine[k, 0, 0] = top
+        mine[k, 0, 1] = bottom
+        return [
+            send(
+                mine.at[k, 0],
+                tile_in.at[k, d - 1],
+                t_s.at[k, d - 1],
+                t_r.at[k, d - 1],
+                at(lax.rem(me + d, n)),
+            )
+            for d in range(1, n)
+        ]
+
+    def slab_round(k, copies):
+        total = mine[k, 0]
+        for d in range(1, n):
+            copies[d - 1].wait_recv()
+            total += tile_in[k, d - 1]
+        mine[k, 1] = total
+        return [
+            send(
+                mine.at[k, 1],
+                slab_in.at[k, d - 1],
+                b_s.at[k, d - 1],
+                b_r.at[k, d - 1],
+                along(lax.rem(slab + d, slabs)),
+            )
+            for d in range(1, slabs)
+        ]
+
+    def end_round(k, copies):
+        total = mine[k, 1]
+        for d in range(1, slabs):
+            copies[d - 1].wait_recv()
+            total += slab_in[k, d - 1]
+        sums[k] = total
+        return total
+
+    if mode == "last":
+        up = send(halo.at[0], halo_in.at[0], h_s.at[0], h_r.at[0], along(lax.rem(slab + 1, slabs)))
+        down = send(
+            halo.at[1], halo_in.at[1], h_s.at[1], h_r.at[1], along(lax.rem(slab + slabs - 1, slabs))
+        )
+        curve = jnp.zeros((8, LANES), f32)
+        for g in range(pieces):
+            value = projected[g]
+            curve += fold8(weights[:, g * LANES : (g + 1) * LANES] * value * value)
+        round0 = tile_round(0, square[...], curve)
     second_hop = []
     for c, span in enumerate(spans):
         first_hop[c].wait_recv()
@@ -265,11 +324,15 @@
             ]
         )
     if mode == "last":
-        up = send(halo.at[0], halo_in.at[0], h_s.at[0], h_r.at[0], along(lax.rem(slab + 1, slabs)))
-        down = send(
-            halo.at[1], halo_in.at[1], h_s.at[1], h_r.at[1], along(lax.rem(slab + slabs - 1, slabs))
-        )
-    curve = jnp.zeros((8, LANES), f32)
+        total = end_round(0, slab_round(0, round0))
+        rate = jnp.sum(total[0]) / jnp.sum(total[1])
+
+        def add_square(p, carry):
+            value = first[p] - rate * turned[p]
+            return carry + fold8(value * value)
+
+        squares = lax.fori_loop(0, first.shape[0], add_square, jnp.zeros((8, LANES), f32))
+        curve = jnp.zeros((8, LANES), f32)
     across = []
     aside = []
     for c, span in enumerate(spans):
@@ -282,9 +345,11 @@
             lanes = slice(g * LANES, (g + 1) * LANES)
             if mode == "first":
                 value = value - measured[:, lanes]
+            if mode == "last":
+                value = projected[g] - rate * value
             weighted = weights[:, lanes] * value
             own[g] = value
-            if mode != "first":
+            if mode == "last":
                 curve += fold8(weighted * value)
             if mode != "last":
                 gathered[row, par, g] = weighted
@@ -297,45 +362,14 @@
                 ]
             )
             aside.append(send(spot, spot, sib_s.at[0, c], sib_r.at[0, c], at(sibling)))
-    if mode != "first":
-        mine[0, 0] = square[...]
-        mine[0, 1] = curve
-        tile_copies = [
-            send(
-                mine.at[0],
-                tile_in.at[d - 1],
-                t_s.at[d - 1],
-                t_r.at[d - 1],
-                at(lax.rem(me + d, n)),
-            )
-            for d in range(1, n)
-        ]
     if mode != "last":
         for c, span in enumerate(spans):
             for d in range(1, half):
                 across[c][d - 1].wait_recv()
                 spot = gathered.at[lax.rem(row + half - d, half), par, span]
                 aside.append(send(spot, spot, sib_s.at[d, c], sib_r.at[d, c], at(sibling)))
-    if mode != "first":
-        total = mine[0]
-        for d in range(1, n):
-            tile_copies[d - 1].wait_recv()
-            total += tile_in[d - 1]
-        mine[1] = total
-        slab_copies = [
-            send(
-                mine.at[1],
-                slab_in.at[d - 1],
-                b_s.at[d - 1],
-                b_r.at[d - 1],
-                along(lax.rem(slab + d, slabs)),
-            )
-            for d in range(1, slabs)
-        ]
-        for d in range(1, slabs):
-            slab_copies[d - 1].wait_recv()
-            total += slab_in[d - 1]
-        sums[...] = total
+    if mode == "last":
+        end_round(1, slab_round(1, tile_round(1, squares, curve)))
     for copy in aside:
         copy.wait_recv()
     if mode == "last":
@@ -353,10 +387,9 @@
     outs = [shape((pieces, slices, LANES), f32)]
     if mode != "last":
         outs.append(shape((half, 2, pieces, slices, LANES), f32))
-    if mode != "first":
-        outs.append(shape((2, 8, LANES), f32))
-    if mode == "last":
-        outs.append(shape(extra[1].shape, f32))
+    if mode == "last":
+        outs.append(shape((2, 2, 8, LANES), f32))
+        outs.append(shape(extra[-1].shape, f32))
     dma = pltpu.SemaphoreType.DMA
     others = max(half - 1, 1)
     scratch = [
@@ -372,18 +405,19 @@
         dma((half, chunks)),
         dma((half, chunks)),
     ]
-    if mode != "first":
+    if mode == "last":
+        around = max(slabs - 1, 1)
         scratch += [
-            pltpu.VMEM((2, 2, 8, LANES), f32),
-            pltpu.VMEM((n - 1, 2, 8, LANES), f32),
-            pltpu.VMEM((max(slabs - 1, 1), 2, 8, LANES), f32),
-            dma((n - 1,)),
-            dma((n - 1,)),
-            dma((max(slabs - 1, 1),)),
-            dma((max(slabs - 1, 1),)),
+            pltpu.VMEM((2, 2, 2, 8, LANES), f32),
+            pltpu.VMEM((2, n - 1, 2, 8, LANES), f32),
+            pltpu.VMEM((2, around, 2, 8, LANES), f32),
+            dma((2, n - 1)),
+            dma((2, n - 1)),
+            dma((2, around)),
+            dma((2, around)),
+            dma((2,)),
+            dma((2,)),
         ]
-    if mode == "last":
-        scratch += [dma((2,)), dma((2,))]
     inputs = [part.reshape(half, 2, pieces, slices, LANES), weights, *extra]
     return pl.pallas_call(
         functools.partial(exchange_kernel, mode, n, slabs, chunks),
@@ -434,20 +468,21 @@
         fs,
         wr.reshape(groups, slices, LANES),
     )
-    projected, wp, sums = exchange("middle", part, weights, [square], n, slabs, 2)
-    halo_shape = shape((2, 2, PASSES, blocks, LANES), f32)
-    grad, part, square, current, halo = local(
+    projected, wp = exchange("middle", part, weights, [], n, slabs, 2)
+    halo_shape = shape((2, 3, PASSES, blocks, LANES), f32)
+    turned, part, halo = local(
         last_kernel,
         "gradient_second",
-        [grad_shape, part_shape, shape((8, LANES), f32), grad_shape, halo_shape],
+        [grad_shape, part_shape, halo_shape],
         [v3],
         fs,
         wp.reshape(groups, slices, LANES),
         first,
         volume,
-        sums,
     )
-    later, last_sums, halo_in = exchange("last", part, weights, [square, halo], n, slabs, 3)
+    later, sums, halo_in = exchange(
+        "last", part, weights, [projected, square, first, turned, halo], n, slabs, 3
+    )
     return pl.pallas_call(
         finish_kernel,
         out_shape=[shape(volume.shape, f32), shape(measured.shape, f32)],
@@ -455,7 +490,7 @@
         out_specs=[VMEM] * 2,
         scratch_shapes=[pltpu.VMEM((blocks, slices + 16, LANES), f32)],
         name="smooth",
-    )(current, grad, halo_in, last_sums, sums, start, projected, later)
+    )(volume, first, turned, halo_in, sums, start, projected, later)
 
 
 def solution(mesh):

time: 103 us -> 96.1 us (0.933)
  Pallas kernels: 102 us -> 95.2 us
    pallas_call x3, Pallas kernels: 66.6 us -> 62.8 us  [exchange(): pl.pallas_call(functools.partial(exchange_kernel, mode, n, slabs, chunks)...]
    pallas_call x3, Pallas kernels: 31.8 us -> 28.7 us  [local(): pl.pallas_call(body, out_shape=outs, in_specs=[SMEM, SMEM] + [VMEM] * len...]
where the time goes in v3:
time: 96.1 us; the launch traced here: 95.8 us
  Pallas kernels  95.2 us (99%)
    pallas_call x3, Pallas kernels, exchange(): pl.pallas_call(functools.partial(exchange_kernel, mode, n, slabs, chunks)...  62.8 us
    pallas_call x3, Pallas kernels, local(): pl.pallas_call(body, out_shape=outs, in_specs=[SMEM, SMEM] + [VMEM] * len...  28.7 us
    pallas_call x1, Pallas kernels, shards(): pl.pallas_call(finish_kernel, out_shape=[shape(volume.shape, f32), shape(...  3.65 us

profile of v3, /device:TPU:0, one launch (start us, length us, event | category | flops | bytes accessed | tf_op | source)
XLA Modules:
  0.0 95.8 jit_solution(8334198403601207526)
XLA Ops:
  0.6 8.7 %project_first.1 = (bf16[64,128,256]{2,1,0:T(8,128)(2,1)}, f32[64,32,128]{2,1,0:T(8,128)}) custom-call(s32[256]{0:T(256)} %pix.5, s32[256]{0:T(256)} %strip.5, f32[32,4096]{1,0:T(8,128)} %volume.5, f32[64,128,128]{2,1,0:T(8,128)} %bitcast.6), custom_call_target="tpu_custom_call" | custom-call | tf_op jit(solution)/shard_map/project_first/pallas_call | solution.py:445
  9.3 20.1 %exchange_first.1 = (f32[16,32,128]{2,1,0:T(8,128)}, f32[2,2,16,32,128]{4,3,2,1,0:T(8,128)}) custom-call(f32[2,2,16,32,128]{4,3,2,1,0:T(8,128)} %bitcast.9, f32[32,2048]{1,0:T(8,128)} %refs_1_.5, f32[32,2048]{1,0:T(8,128)} %refs_2_.1), custom_call_target="tpu_custom_call" | custom-call | tf_op jit(solution)/shard_map/exchange_first/pallas_call | solution.py:422
  29.5 9.8 %gradient_first.1 = (f32[32,32,128]{2,1,0:T(8,128)}, f32[64,32,128]{2,1,0:T(8,128)}, f32[8,128]{1,0:T(8,128)}) custom-call(s32[256]{0:T(256)} %pix.5, s32[256]{0:T(256)} %strip.5, bf16[64,128,256]{2,1,0:T(8,128)(2,1)} %get-tuple-element.17.fs, f32[64,32,128]{2,1,0:T(8,128)} %bitcast.7), custom_call_target="tpu_custom_call" | custom-call | tf_op jit(solution)/shard_map/gradient_first/pallas_call | solution.py:445
  39.2 19.1 %exchange_middle.1 = (f32[16,32,128]{2,1,0:T(8,128)}, f32[2,2,16,32,128]{4,3,2,1,0:T(8,128)}) custom-call(f32[2,2,16,32,128]{4,3,2,1,0:T(8,128)} %bitcast.8, f32[32,2048]{1,0:T(8,128)} %refs_1_.5), custom_call_target="tpu_custom_call" | custom-call | tf_op jit(solution)/shard_map/exchange_middle/pallas_call | solution.py:422
  58.4 10.2 %gradient_second.1 = (f32[32,32,128]{2,1,0:T(8,128)}, f32[64,32,128]{2,1,0:T(8,128)}, f32[2,3,3,32,128]{4,3,2,1,0:T(8,128)}) custom-call(s32[256]{0:T(256)} %pix.5, s32[256]{0:T(256)} %strip.5, bf16[64,128,256]{2,1,0:T(8,128)(2,1)} %get-tuple-element.17.fs, f32[64,32,128]{2,1,0:T(8,128)} %bitcast.11, f32[32,32,128]{2,1,0:T(8,128)} %get-tuple-element.20.first.refs_4_, ...), custom_call_target="tpu_custom_call" | custom-call | tf_op jit(solution)/shard_map/gradient_second/pallas_call | solution.py:445
  68.6 23.6 %exchange_last.1 = (f32[16,32,128]{2,1,0:T(8,128)}, f32[2,2,8,128]{3,2,1,0:T(8,128)}, f32[2,3,3,32,128]{4,3,2,1,0:T(8,128)}) custom-call(f32[2,2,16,32,128]{4,3,2,1,0:T(8,128)} %bitcast.10, f32[32,2048]{1,0:T(8,128)} %refs_1_.5, f32[16,32,128]{2,1,0:T(8,128)} %get-tuple-element.25.refs_2_.projected, f32[8,128]{1,0:T(8,128)} %get-tuple-element.26.refs_3_, ...), custom_call_target="tpu_custom_call" | custom-call | tf_op jit(solution)/shard_map/exchange_last/pallas_call | solution.py:422
  92.2 3.7 %smooth.1 = (f32[32,4096]{1,0:T(8,128)}, f32[32,2048]{1,0:T(8,128)}) custom-call(f32[32,4096]{1,0:T(8,128)} %volume.5, f32[32,32,128]{2,1,0:T(8,128)} %get-tuple-element.20.first.refs_4_, f32[32,32,128]{2,1,0:T(8,128)} %get-tuple-element.23.refs_5_.turned, f32[2,3,3,32,128]{4,3,2,1,0:T(8,128)} %get-tuple-element.28.halo, ...), custom_call_target="tpu_custom_call" | custom-call | tf_op jit(solution)/shard_map/smooth/pallas_call | solution.py:486

commit v4 on v3

--- a/solution.py
+++ b/solution.py
@@ -10,8 +10,9 @@
 STRIPS = 256
 PASSES = 3
 LANES = 128
-UNROLL = 16
-MOST_CHUNKS = 4
+UNROLL = 32
+STAGE = 16
+MOST_CHUNKS = 8
 
 huber_width = 0.5
 smooth_rate = 0.2
@@ -32,26 +33,28 @@
     return jnp.concatenate([high, low, high], axis=1)
 
 
-def project(v3, fs, pix, strip, part):
+def project(v3, fs, pix, strip, part, stage=0, stages=1):
     slices = v3.shape[1]
-    slots = pix.shape[0] // fs.shape[0]
+    slots = pix.shape[0] // (fs.shape[0] * stages)
+    base = stage * fs.shape[0]
     rows = LANES // slots
     slot_of = lax.broadcasted_iota(jnp.int32, (slices, LANES), 1) // rows
-    part[...] = jnp.zeros_like(part)
+
+    unroll = min(UNROLL, fs.shape[0])
 
     def step(i, carry):
         found = []
-        for u in range(UNROLL):
-            t = i * UNROLL + u
+        for u in range(unroll):
+            t = i * unroll + u
             pair = fs[t]
             high, low = pair[:, :LANES], pair[:, LANES:]
             right = jnp.concatenate([high, high, low], axis=1)
-            left = jnp.concatenate([v3[pix[t * slots + k]] for k in range(slots)], axis=0)
+            left = jnp.concatenate([v3[pix[(base + t) * slots + k]] for k in range(slots)], axis=0)
             out = lax.dot_general(
                 left, right, (((1,), (1,)), ((), ())), preferred_element_type=f32
             )
             for k in range(slots):
-                q = strip[t * slots + k]
+                q = strip[(base + t) * slots + k]
                 own = lax.bitwise_and(q, slots - 1)
                 turned = pltpu.roll(
                     out[k * slices : (k + 1) * slices],
@@ -68,7 +71,7 @@
             part[g] += out
         return carry
 
-    lax.fori_loop(0, fs.shape[0] // UNROLL, step, 0)
+    lax.fori_loop(0, fs.shape[0] // unroll, step, 0)
 
 
 def back(wr, fs, pix, strip, grad):
@@ -78,10 +81,12 @@
     slot_of = lax.broadcasted_iota(jnp.int32, (slices, LANES), 1) // rows
     grad[...] = jnp.zeros_like(grad)
 
+    unroll = min(UNROLL, fs.shape[0])
+
     def step(i, carry):
         found = []
-        for u in range(UNROLL):
-            t = i * UNROLL + u
+        for u in range(unroll):
+            t = i * unroll + u
             pair = fs[t]
             high, low = pair[:, :LANES], pair[:, LANES:]
             right = jnp.concatenate([high, high, low], axis=0)
@@ -106,21 +111,21 @@
             grad[p] += out
         return carry
 
-    lax.fori_loop(0, fs.shape[0] // UNROLL, step, 0)
-
-
-def first_kernel(pix, strip, volume, feet, fs, part, v3):
-    for p in range(v3.shape[0]):
-        v3[p] = triple(volume[:, p * LANES : (p + 1) * LANES])
-
-    def split(i, carry):
-        for u in range(UNROLL):
-            t = i * UNROLL + u
-            fs[t] = jnp.concatenate(halves(feet[t]), axis=1)
-        return carry
-
-    lax.fori_loop(0, feet.shape[0] // UNROLL, split, 0)
-    project(v3, fs, pix, strip, part)
+    lax.fori_loop(0, fs.shape[0] // unroll, step, 0)
+
+
+def first_kernel(stages, pix, strip, volume, feet, fs, part, v3):
+    stage = pl.program_id(0)
+
+    @pl.when(stage == 0)
+    def _():
+        part[...] = jnp.zeros_like(part)
+        for p in range(v3.shape[0]):
+            v3[p] = triple(volume[:, p * LANES : (p + 1) * LANES])
+
+    for t in range(feet.shape[0]):
+        fs[t] = jnp.concatenate(halves(feet[t]), axis=1)
+    project(v3, fs, pix, strip, part, stage, stages)
 
 
 def fold8(x):
@@ -135,6 +140,7 @@
         v3[p] = triple(value)
         total += fold8(value * value)
     square[...] = total
+    part[...] = jnp.zeros_like(part)
     project(v3, fs, pix, strip, part)
 
 
@@ -152,6 +158,7 @@
                 ]
             halo[side, 1, row] = first[:, spot, :]
             halo[side, 2, row] = grad[:, spot, :]
+    part[...] = jnp.zeros_like(part)
     project(v3, fs, pix, strip, part)
 
 
@@ -296,10 +303,6 @@
         return total
 
     if mode == "last":
-        up = send(halo.at[0], halo_in.at[0], h_s.at[0], h_r.at[0], along(lax.rem(slab + 1, slabs)))
-        down = send(
-            halo.at[1], halo_in.at[1], h_s.at[1], h_r.at[1], along(lax.rem(slab + slabs - 1, slabs))
-        )
         curve = jnp.zeros((8, LANES), f32)
         for g in range(pieces):
             value = projected[g]
@@ -324,7 +327,12 @@
             ]
         )
     if mode == "last":
-        total = end_round(0, slab_round(0, round0))
+        round0 = slab_round(0, round0)
+        up = send(halo.at[0], halo_in.at[0], h_s.at[0], h_r.at[0], along(lax.rem(slab + 1, slabs)))
+        down = send(
+            halo.at[1], halo_in.at[1], h_s.at[1], h_r.at[1], along(lax.rem(slab + slabs - 1, slabs))
+        )
+        total = end_round(0, round0)
         rate = jnp.sum(total[0]) / jnp.sum(total[1])
 
         def add_square(p, carry):
@@ -451,14 +459,25 @@
             name=name,
         )(foot_pixel, foot_strip, *inputs)
 
-    fs, part = local(
-        first_kernel,
-        "project_first",
-        [shape((count // slots, LANES, 2 * LANES), bf16), part_shape],
-        [v3],
-        volume,
-        footprints.reshape(count // slots, LANES, LANES),
-    )
+    size = min(STAGE, count // slots)
+    stages = count // slots // size
+    fs, part = pl.pallas_call(
+        functools.partial(first_kernel, stages),
+        grid=(stages,),
+        out_shape=[shape((count // slots, LANES, 2 * LANES), bf16), part_shape],
+        in_specs=[
+            SMEM,
+            SMEM,
+            pl.BlockSpec(volume.shape, lambda i: (0, 0)),
+            pl.BlockSpec((size, LANES, LANES), lambda i: (i, 0, 0)),
+        ],
+        out_specs=[
+            pl.BlockSpec((size, LANES, 2 * LANES), lambda i: (i, 0, 0)),
+            pl.BlockSpec(part_shape.shape, lambda i: (0, 0, 0)),
+        ],
+        scratch_shapes=[v3],
+        name="project_first",
+    )(foot_pixel, foot_strip, volume, footprints.reshape(count // slots, LANES, LANES))
     start, wr = exchange("first", part, weights, [measured], n, slabs, 1)
     first, part, square = local(
         middle_kernel,

time: 96.1 us -> 93.3 us (0.971)
  Pallas kernels: 95.2 us -> 92.4 us
    pallas_call x3 -> x2, Pallas kernels: 28.7 us -> 18.3 us  [local(): pl.pallas_call(body, out_shape=outs, in_specs=[SMEM, SMEM] + [VMEM] * len...]
    pallas_call x0 -> x1, Pallas kernels: none -> 7.07 us  [shards(): pl.pallas_call(functools.partial(first_kernel, stages), grid=(stages,), o...]
where the time goes in v4:
time: 93.3 us; the launch traced here: 93 us
  Pallas kernels  92.4 us (99%)
    pallas_call x3, Pallas kernels, exchange(): pl.pallas_call(functools.partial(exchange_kernel, mode, n, slabs, chunks)...  63.4 us
    pallas_call x2, Pallas kernels, local(): pl.pallas_call(body, out_shape=outs, in_specs=[SMEM, SMEM] + [VMEM] * len...  18.3 us
    pallas_call x1, Pallas kernels, shards(): pl.pallas_call(functools.partial(first_kernel, stages), grid=(stages,), o...  7.07 us
    pallas_call x1, Pallas kernels, shards(): pl.pallas_call(finish_kernel, out_shape=[shape(volume.shape, f32), shape(...  3.65 us

profile of v4, /device:TPU:0, one launch (start us, length us, event | category | flops | bytes accessed | tf_op | source)
XLA Modules:
  0.0 93.0 jit_solution(4190157170874460676)
XLA Ops:
  0.6 7.1 %project_first.1 = (bf16[64,128,256]{2,1,0:T(8,128)(2,1)}, f32[64,32,128]{2,1,0:T(8,128)}) custom-call(s32[256]{0:T(256)} %pix.5, s32[256]{0:T(256)} %strip.5, f32[32,4096]{1,0:T(8,128)} %volume.5, f32[64,128,128]{2,1,0:T(8,128)} %bitcast.6), custom_call_target="tpu_custom_call" | custom-call | tf_op jit(solution)/shard_map/project_first/pallas_call | solution.py:464
  7.7 20.4 %exchange_first.1 = (f32[16,32,128]{2,1,0:T(8,128)}, f32[2,2,16,32,128]{4,3,2,1,0:T(8,128)}) custom-call(f32[2,2,16,32,128]{4,3,2,1,0:T(8,128)} %bitcast.9, f32[32,2048]{1,0:T(8,128)} %refs_1_.5, f32[32,2048]{1,0:T(8,128)} %refs_2_.1), custom_call_target="tpu_custom_call" | custom-call | tf_op jit(solution)/shard_map/exchange_first/pallas_call | solution.py:430
  28.1 8.9 %gradient_first.1 = (f32[32,32,128]{2,1,0:T(8,128)}, f32[64,32,128]{2,1,0:T(8,128)}, f32[8,128]{1,0:T(8,128)}) custom-call(s32[256]{0:T(256)} %pix.5, s32[256]{0:T(256)} %strip.5, bf16[64,128,256]{2,1,0:T(8,128)(2,1)} %get-tuple-element.17.fs, f32[64,32,128]{2,1,0:T(8,128)} %bitcast.7), custom_call_target="tpu_custom_call" | custom-call | tf_op jit(solution)/shard_map/gradient_first/pallas_call | solution.py:453
  37.0 19.3 %exchange_middle.1 = (f32[16,32,128]{2,1,0:T(8,128)}, f32[2,2,16,32,128]{4,3,2,1,0:T(8,128)}) custom-call(f32[2,2,16,32,128]{4,3,2,1,0:T(8,128)} %bitcast.8, f32[32,2048]{1,0:T(8,128)} %refs_1_.5), custom_call_target="tpu_custom_call" | custom-call | tf_op jit(solution)/shard_map/exchange_middle/pallas_call | solution.py:430
  56.3 9.4 %gradient_second.1 = (f32[32,32,128]{2,1,0:T(8,128)}, f32[64,32,128]{2,1,0:T(8,128)}, f32[2,3,3,32,128]{4,3,2,1,0:T(8,128)}) custom-call(s32[256]{0:T(256)} %pix.5, s32[256]{0:T(256)} %strip.5, bf16[64,128,256]{2,1,0:T(8,128)(2,1)} %get-tuple-element.17.fs, f32[64,32,128]{2,1,0:T(8,128)} %bitcast.11, f32[32,32,128]{2,1,0:T(8,128)} %get-tuple-element.20.first.refs_4_, ...), custom_call_target="tpu_custom_call" | custom-call | tf_op jit(solution)/shard_map/gradient_second/pallas_call | solution.py:453
  65.7 23.6 %exchange_last.1 = (f32[16,32,128]{2,1,0:T(8,128)}, f32[2,2,8,128]{3,2,1,0:T(8,128)}, f32[2,3,3,32,128]{4,3,2,1,0:T(8,128)}) custom-call(f32[2,2,16,32,128]{4,3,2,1,0:T(8,128)} %bitcast.10, f32[32,2048]{1,0:T(8,128)} %refs_1_.5, f32[16,32,128]{2,1,0:T(8,128)} %get-tuple-element.25.refs_2_.projected, f32[8,128]{1,0:T(8,128)} %get-tuple-element.26.refs_3_, ...), custom_call_target="tpu_custom_call" | custom-call | tf_op jit(solution)/shard_map/exchange_last/pallas_call | solution.py:430
  89.4 3.7 %smooth.1 = (f32[32,4096]{1,0:T(8,128)}, f32[32,2048]{1,0:T(8,128)}) custom-call(f32[32,4096]{1,0:T(8,128)} %volume.5, f32[32,32,128]{2,1,0:T(8,128)} %get-tuple-element.20.first.refs_4_, f32[32,32,128]{2,1,0:T(8,128)} %get-tuple-element.23.refs_5_.turned, f32[2,3,3,32,128]{4,3,2,1,0:T(8,128)} %get-tuple-element.28.halo, ...), custom_call_target="tpu_custom_call" | custom-call | tf_op jit(solution)/shard_map/smooth/pallas_call | solution.py:505
